TPU v7x, 256 devices: a whole 4x4x8 slice. The times are simulated.
256 devices in a mesh: tok: 64 (over y, z, core), grp: 4 (over x).
Axes of the slice: x: 4, y: 4, z: 8, core: 2. Of those that a mesh axis runs over, the one named last changes fastest.
Arguments:
- tokens: bfloat16 [98304, 1024], P(('tok', 'grp')), may hold values from -6 to 6
- norm_gain: float32 [1024], replicated, may hold values from 0.25 to 1.75
- input_weight: bfloat16 [1024, 3072], P('tok', 'grp')
- output_weight: bfloat16 [1024, 1024], P('tok', 'grp'), may hold values from -2 to 2
- segment_ids: int32 [98304], replicated, may hold values from 0 to 191, never falling along the last dimension, each value on 1 to 1024 neighbouring positions
- page_owner: int32 [24576, 1], P(('tok', 'grp')), may hold values from 0 to 63; in each aligned block of 96 rows (0 to 95, 96 to 191, ...) at most 3 rows name the same one
Outputs:
- attended: bfloat16 [98304, 1024], P(('tok', 'grp'))
- cache_pages: bfloat16 [49152, 8192], P(('tok', 'grp'))
Inputs may be any that keep to these rules, and one draw needn't show every extreme that they name: `segment_ids`: segment ids never fall along the pack; every id occurs on 1 to 1024 consecutive tokens, and some document has exactly 1024 tokens. `page_owner`: within the 96 pages of one device no owner is named more than 3 times, and in some device one owner is named exactly 3 times.
All inputs are finite; a program needn't handle non-finite values.
Results may differ from a plain program's by a relative error of at most 0.0089.
Values may be sent and summed in bfloat16 or wider, within the bound.
A program may use at most 128 MiB of HBM per device.

v0:
```python
import jax
import jax.numpy as jnp
from jax import lax
from jax.sharding import PartitionSpec as P

H = 16
SPAN = 1024
PAGE = 4
NEG_FILL = -1e30
ROPE_BASE = 160000.0
EPSILON = 1e-05


def shifted(value, axis, steps):
    count = lax.axis_size(axis)
    initial, last = (max(0, -steps), min(count, count - steps))
    return lax.ppermute(value, axis, [(source, source + steps) for source in range(initial, last)])


def layer_norm(tokens, norm_gain):
    values = tokens.astype(jnp.float32)
    center = jnp.mean(values, axis=-1, keepdims=True)
    spread = jnp.mean(jnp.square(values - center), axis=-1, keepdims=True)
    return ((values - center) * lax.rsqrt(spread + EPSILON) * norm_gain).astype(jnp.bfloat16)


def rotate(block_part, positions, head_count):
    row_count = block_part.shape[0]
    head_dim = block_part.shape[1] // head_count
    half_dim = head_dim // 2
    shaped = block_part.reshape(row_count, head_count, head_dim)
    inverse = 1.0 / ROPE_BASE ** (jnp.arange(half_dim, dtype=jnp.float32) * 2.0 / head_dim)
    angles = positions.astype(jnp.float32)[:, None] * inverse[None, :]
    cosine = jnp.concatenate([jnp.cos(angles), jnp.cos(angles)], axis=1)[:, None, :]
    sine_table = jnp.concatenate([jnp.sin(angles), jnp.sin(angles)], axis=1)[:, None, :]
    turned = jnp.concatenate([-shaped[..., half_dim:], shaped[..., :half_dim]], axis=-1)
    return (
        (shaped * cosine + turned * sine_table)
        .reshape(row_count, head_count * head_dim)
        .astype(jnp.bfloat16)
    )


def positions_of(segment_ids, own_ids, first_row):
    starts = jnp.searchsorted(segment_ids, own_ids, side="left")
    return first_row + jnp.arange(own_ids.shape[0], dtype=jnp.int32) - starts


def pair_scores(query_pair, key_pair, score_scale):
    return (
        jnp.einsum("tnd,snd->nts", query_pair, key_pair, preferred_element_type=jnp.float32)
        * score_scale
    )


def attend_pairs(queries, key_window, value_window, allowed, head_count):
    row_count = queries.shape[0]
    window_len = key_window.shape[0]
    head_dim = queries.shape[1] // head_count
    pair_count = head_count // 2
    score_scale = head_dim ** (-0.5)
    query_stack = jnp.transpose(queries.reshape(row_count, pair_count, 2, head_dim), (1, 0, 2, 3))
    key_stack = jnp.transpose(key_window.reshape(window_len, pair_count, 2, head_dim), (1, 0, 2, 3))
    value_stack = jnp.transpose(
        value_window.reshape(window_len, pair_count, 2, head_dim), (1, 0, 2, 3)
    )

    def one_pair(operands):
        query_pair, key_pair, value_pair = operands
        scores = jnp.where(allowed[None], pair_scores(query_pair, key_pair, score_scale), NEG_FILL)
        row_peak = jnp.max(scores, axis=-1, keepdims=True)
        exponent = jnp.exp(scores - row_peak)
        row_total = jnp.sum(exponent, axis=-1)
        weights = exponent.astype(jnp.bfloat16)
        mixed_rows = jnp.einsum(
            "nts,snd->tnd", weights, value_pair, preferred_element_type=jnp.float32
        )
        return mixed_rows / jnp.transpose(row_total)[:, :, None]

    mixed_stack = lax.map(one_pair, (query_stack, key_stack, value_stack))
    return (
        jnp.transpose(mixed_stack, (1, 0, 2, 3))
        .reshape(row_count, head_count * head_dim)
        .astype(jnp.bfloat16)
    )


def per_device(tokens, norm_gain, input_weight, output_weight, segment_ids, page_owner):
    row_count = tokens.shape[0]
    model_width = tokens.shape[1]
    device = lax.axis_index(("tok", "grp"))
    first_row = device * row_count
    normed = layer_norm(tokens, norm_gain)
    input_cols, output_cols = (
        lax.all_gather(input_weight, "grp", axis=1, tiled=True),
        lax.all_gather(output_weight, "grp", axis=1, tiled=True),
    )
    section = normed
    joined = jnp.dot(
        section,
        lax.all_gather(input_cols, "tok", axis=0, tiled=True),
        preferred_element_type=jnp.float32,
    )
    own_ids = lax.dynamic_slice_in_dim(segment_ids, first_row, row_count, 0)
    positions = positions_of(segment_ids, own_ids, first_row)
    queries = rotate(joined[:, :model_width], positions, H)
    key_rows = rotate(joined[:, model_width : 2 * model_width], positions, H)
    value_rows = joined[:, 2 * model_width :].astype(jnp.bfloat16)
    paired = jnp.stack([key_rows, value_rows])
    reach_blocks = (SPAN + row_count - 2) // row_count
    window_len = (2 * reach_blocks + 1) * row_count
    earlier = [shifted(paired, ("tok", "grp"), distance) for distance in range(reach_blocks, 0, -1)]
    later_blocks = [
        shifted(paired, ("tok", "grp"), -distance) for distance in range(1, reach_blocks + 1)
    ]
    window = jnp.concatenate(earlier + [paired] + later_blocks, axis=1)
    filler = jnp.full((reach_blocks * row_count,), -1, jnp.int32)
    padded_ids = jnp.concatenate([filler, segment_ids, filler])
    window_ids = lax.dynamic_slice_in_dim(padded_ids, first_row, window_len, 0)
    allowed = own_ids[:, None] == window_ids[None, :]
    mixed_rows = attend_pairs(queries, window[0], window[1], allowed, H)
    section = mixed_rows
    attended = jnp.dot(
        section,
        lax.all_gather(output_cols, "tok", axis=0, tiled=True),
        preferred_element_type=jnp.float32,
    ).astype(jnp.bfloat16)
    page_rows = jnp.concatenate([key_rows, value_rows], axis=1).reshape(
        row_count // PAGE, 2 * PAGE * model_width
    )
    owners = page_owner[:, 0]
    page_count = owners.shape[0]
    earlier_mask = jnp.arange(page_count)[:, None] > jnp.arange(page_count)[None, :]
    page_ranks = jnp.sum(
        ((owners[:, None] == owners[None, :]) & earlier_mask).astype(jnp.int32), axis=1
    )
    peer_count = lax.axis_size("tok")
    capacity = max(2, (2 * page_count + peer_count - 1) // peer_count)
    send_slots = jnp.zeros((peer_count * capacity, page_rows.shape[1]), jnp.bfloat16)
    send_slots = send_slots.at[owners * capacity + page_ranks].set(page_rows)
    cache_pages = lax.all_to_all(send_slots, "tok", split_axis=0, concat_axis=0, tiled=True)
    return (attended, cache_pages)


def solution(mesh):
    placed = (
        P(("tok", "grp"), None),
        P(),
        P("tok", "grp"),
        P("tok", "grp"),
        P(),
        P(("tok", "grp"), None),
    )
    return jax.shard_map(
        per_device,
        mesh=mesh,
        in_specs=placed,
        out_specs=(P(("tok", "grp"), None), P(("tok", "grp"), None)),
        check_vma=False,
    )
```

profile of v0, /device:TPU:1, one launch (start us, length us, event | category | flops | bytes accessed | tf_op | source)
XLA Modules:
  0.0 458.8 jit_solution(4806925202576879841)
XLA Ops:
  7.2 12.0 %all_gather.12 = bf16[16,3072]{1,0:T(8,128)(2,1)} all-gather(bf16[16,768]{1,0:T(8,128)(2,1)} %param.12), channel_id=1, replica_groups=mesh['tok'=64,'grp'=4] {'grp'}, dimensions={1}, use_global_device_ids=true | all-gather | bytes 122880 | tf_op jit(solution)/shard_map/all_gather | solution.py:95
  20.1 64.1 %while.36 = (s32[]{:T(128)}, u32[384]{0:T(512)S(1)}, u32[384]{0:T(512)S(1)}, s32[98304]{0:T(1024)}, s32[384]{0:T(512)S(1)}, /*index=5*/s32[]{:T(128)}, s32[]{:T(128)}, s32[]{}) while((s32[]{:T(128)}, u32[384]{0:T(512)S(1)}, u32[384]{0:T(512)S(1)}, s32[98304]{0:T(1024)}, s32[384]{0:T(512)S(1)}, /*index=5*/s32[]{:T(128)}, s32[]{:T(128)}, ...), condition=%wide.region_3.4_spmd.clone, body=%wide.region_2.3_spmd.clone.sunk | while | flops 7940 | bytes 31085 | solution.py:45
  20.1 3.7 gather_fusion
  23.8 3.7 gather_fusion
  27.6 3.7 gather_fusion
  31.4 3.7 gather_fusion
  35.2 3.7 gather_fusion
  38.9 3.7 gather_fusion
  42.7 3.7 gather_fusion
  46.5 3.7 gather_fusion
  50.2 3.7 gather_fusion
  54.0 3.7 gather_fusion
  57.8 3.7 gather_fusion
  61.5 3.7 gather_fusion
  65.3 3.7 gather_fusion
  69.1 3.7 gather_fusion
  72.8 3.8 gather_fusion
  76.7 3.7 gather_fusion
  80.5 3.7 gather_fusion
  88.8 16.0 %all-gather.3.cloned.1.call-done = bf16[1024,3072]{1,0:T(8,128)(2,1)} async-done(((bf16[16,3072]{1,0:T(8,128)(2,1)}), bf16[1024,3072]{1,0:T(8,128)(2,1)}) %all-gather.3.cloned.1.call-update) | async-done | bytes 6291472 | tf_op jit(solution)/shard_map/all_gather | solution.py:101
  104.8 5.1 %fusion.38 = f32[384,3072]{1,0:T(8,128)S(1)} fusion(bf16[1024,3072]{1,0:T(8,128)(2,1)} %all-gather.3.cloned.1.call-done, bf16[384,1024]{1,0:T(8,128)(2,1)} %param.10, f32[1024]{0:T(1024)S(1)} %copy-done.10, f32[384]{0:T(512)S(1)} %add_rsqrt_fusion, f32[384]{0:T(512)S(1)} %broadcast_multiply_fusion), kind=kOutput, calls=%fused_computation.47 | convolution fusion | flops 2417885184 | bytes 11803648 | tf_op jit(solution)/shard_map/dot_general | solution.py:99
  113.1 3.3 copy.21
  116.5 3.1 copy.25
  123.7 3.1 copy.22
  126.8 3.0 copy.26
  129.8 4.6 %add_convert_fusion = (bf16[384,1024]{1,0:T(8,128)(2,1)}, bf16[384,1024]{1,0:T(8,128)(2,1)S(1)}) fusion(f32[384,1024]{1,0:T(8,128)} %copy.26, f32[384,1024]{1,0:T(8,128)S(1)} %copy.20, f32[384,3072]{1,0:T(8,128)} %copy-done.1, f32[384,1024]{1,0:T(8,128)} %copy.22), kind=kLoop, calls=%fused_computation.44 | loop fusion | flops 2359296 | bytes 9437184 | tf_op jit(solution)/shard_map/convert_element_type | solution.py:40
  135.8 4.3 collective-permute-start
  140.1 3.0 collective-permute-start.1
  143.1 2.5 collective-permute-start.2
  145.6 4.3 collective-permute-start.3
  149.9 3.1 collective-permute-start.4
  153.0 138.8 %all_gather.14 = bf16[16,1024]{1,0:T(8,128)(2,1)} all-gather(bf16[16,256]{1,0:T(8,128)(2,1)S(1)} %copy-done.9), channel_id=1, replica_groups=mesh['tok'=64,'grp'=4] {'grp'}, dimensions={1}, use_global_device_ids=true | all-gather | bytes 40960 | tf_op jit(solution)/shard_map/all_gather | solution.py:96
  297.5 2.4 reshape.75
  299.9 4.8 %scatter_custom_fusion = bf16[192,8192]{1,0:T(8,128)(2,1)S(1)} fusion(s32[96]{0:T(128)} %fusion.46, bf16[96,8192]{1,0:T(8,128)(2,1)} %reshape.75, bf16[]{:T(256)} %constant.92.clone.1), kind=kCustom, calls=%fused_computation.42 | custom fusion | bytes 3146240 | tf_op jit(solution)/shard_map/scatter | solution.py:140
  304.7 4.4 all_to_all.8
  309.1 10.1 %all-to-all-start = ((bf16[64,3,8192]{2,1,0:T(4,128)(2,1)}), bf16[64,3,8192]{2,1,0:T(4,128)(2,1)}, u32[]{:S(2)}, u32[]{:S(2)}) async-start(bf16[64,3,8192]{2,1,0:T(4,128)(2,1)} %all_to_all.8), calls=%async_computation | async-start | bytes 8388608 | tf_op jit(solution)/shard_map/all_to_all | solution.py:141
  319.1 2.7 constant_dynamic-update-slice_fusion.6
  321.9 2.8 constant_dynamic-update-slice_fusion.5
  324.7 2.7 constant_dynamic-update-slice_fusion.4
  328.8 2.8 constant_dynamic-update-slice_fusion.2
  331.6 2.7 constant_dynamic-update-slice_fusion.1
  334.2 2.7 constant_dynamic-update-slice_fusion
  336.9 9.6 %fusion.47 = (bf16[1,2688,1024]{2,1,0:T(8,128)(2,1)}, bf16[1,2688,1024]{2,1,0:T(8,128)(2,1)}) fusion(bf16[2,2688,1024]{2,1,0:T(8,128)(2,1)} %constant_dynamic-update-slice_fusion), kind=kLoop, calls=%fused_computation.79 | loop fusion | bytes 22020096 | tf_op jit(solution)/shard_map/slice | solution.py:121
  346.5 8.0 %copy.28 = bf16[1,2688,1024]{1,2,0:T(8,128)(2,1)} copy(bf16[1,2688,1024]{2,1,0:T(8,128)(2,1)} %get-tuple-element.165) | data formatting | bytes 11010048 | tf_op jit(solution)/shard_map/slice | solution.py:121
  354.5 8.4 %copy.23 = bf16[1,2688,1024]{1,2,0:T(8,128)(2,1)} copy(bf16[1,2688,1024]{2,1,0:T(8,128)(2,1)} %get-tuple-element.166) | data formatting | bytes 11010048 | tf_op jit(solution)/shard_map/slice | solution.py:121
  362.9 78.1 %while.35 = (s32[]{:T(128)}, bf16[8,384,2,64]{1,3,2,0:T(8,128)(2,1)S(1)}, bf16[8,2688,2,64]{1,3,2,0:T(8,128)(2,1)}, bf16[8,384,2,64]{1,3,2,0:T(8,128)(2,1)}, bf1...) while((s32[]{:T(128)}, ...), condition=%wide.region_7.8_spmd.clone, body=%wide.region_4.7_spmd.clone.sunk | while | flops 552270336 | bytes 30602324 | solution.py:80
  363.6 3.2 fusion.59
  369.1 3.6 fusion.61
  373.3 3.2 fusion.59
  378.9 3.6 fusion.61
  383.1 3.2 fusion.59
  388.6 3.6 fusion.61
  392.9 3.2 fusion.59
  398.4 3.6 fusion.61
  402.6 3.2 fusion.59
  408.1 3.6 fusion.61
  412.4 3.2 fusion.59
  417.9 3.6 fusion.61
  422.1 3.2 fusion.59
  427.7 3.6 fusion.61
  431.9 3.2 fusion.59
  437.4 3.6 fusion.61
  441.0 3.5 convolution_convert_fusion
  444.5 7.4 %all_to_all.10 = bf16[192,8192]{1,0:T(8,128)(2,1)} reshape(bf16[64,3,8192]{2,1,0:T(4,128)(2,1)} %all-to-all-done) | data formatting | bytes 6291456 | tf_op jit(solution)/shard_map/all_to_all | solution.py:141
  (165 shorter events, 45.5 us)
Async XLA Ops:
  7.2 97.6 %all-gather.3.cloned.1.call-start = ((), (), s32[]{:S(2)}) async-start(), calls=%async_computation.1 | async-start | bytes 6389760 | tf_op jit(solution)/shard_map/all_gather | solution.py:101
  19.2 421.8 %all-gather.5.cloned.1.call-start = ((), (), s32[]{:S(2)}) async-start(), calls=%async_computation.2 | async-start | bytes 2129920 | tf_op jit(solution)/shard_map/all_gather | solution.py:125
  85.1 19.6 %copy-start.10 = (f32[1024]{0:T(1024)S(1)}, f32[1024]{0:T(1024)}, u32[]{:S(2)}) copy-start(f32[1024]{0:T(1024)} %param.11) | copy-start | bytes 12292
  109.9 3.2 copy-start.1
  113.1 21.3 %copy-start.4 = (bf16[1,384,1024]{2,1,0:T(8,128)(2,1)}, bf16[1,384,1024]{2,1,0:T(8,128)(2,1)S(1)}, u32[]{:S(2)}) copy-start(bf16[1,384,1024]{2,1,0:T(8,128)(2,1)S(1)} %slice_bitcast_fusion) | copy-start | bytes 2359300
  119.5 2.2 copy-start.8
  134.4 162.9 %copy-start.2 = (bf16[384,1024]{1,0:T(8,128)(2,1)}, bf16[384,1024]{1,0:T(8,128)(2,1)S(1)}, u32[]{:S(2)}) copy-start(bf16[384,1024]{1,0:T(8,128)(2,1)S(1)} %get-tuple-element.168) | copy-start | bytes 2359300
  134.4 18.6 %copy-start.9 = (bf16[16,256]{1,0:T(8,128)(2,1)S(1)}, bf16[16,256]{1,0:T(8,128)(2,1)}, u32[]{:S(2)}) copy-start(bf16[16,256]{1,0:T(8,128)(2,1)} %param.13) | copy-start | bytes 24580
  134.5 159.4 %copy-start = (s32[98304]{0:T(1024)S(1)}, s32[98304]{0:T(1024)}, u32[]{:S(2)}) copy-start(s32[98304]{0:T(1024)} %get-tuple-element.315) | copy-start | bytes 1179652
  134.5 159.5 %copy-start.11 = (s32[96,1]{0,1:T(1,128)S(1)}, s32[96,1]{0,1:T(1,128)}, u32[]{:S(2)}) copy-start(s32[96,1]{0,1:T(1,128)} %param.15) | copy-start | bytes 1156
  134.5 161.7 %copy-start.6 = (bf16[384,1024]{1,0:T(8,128)(2,1)S(1)}, bf16[384,1024]{1,0:T(8,128)(2,1)}, u32[]{:S(2)}) copy-start(bf16[384,1024]{1,0:T(8,128)(2,1)} %get-tuple-element.167) | copy-start | bytes 2359300
  135.8 156.1 %collective-permute-start = (bf16[2,384,1024]{2,1,0:T(8,128)(2,1)}, bf16[2,384,1024]{2,1,0:T(8,128)(2,1)}, u32[]{:S(2)}, u32[]{:S(2)}) collective-permute-start(bf16[2,384,1024]{2,1,0:T(8,128)(2,1)} %pad_maximum_fusion), channel_id=1, source_target_pairs={{0,3},{1,4},{2,5},{3,6},{4,7},{5,8},{6,9},{7,10},{8,11},{9,12},{10... | collective-permute-start | bytes 4718600 | tf_op jit(solution)/shard_map/ppermute | solution.py:17
  140.1 181.8 %collective-permute-start.1 = (bf16[2,384,1024]{2,1,0:T(8,128)(2,1)}, bf16[2,384,1024]{2,1,0:T(8,128)(2,1)}, u32[]{:S(2)}, u32[]{:S(2)}) collective-permute-start(bf16[2,384,1024]{2,1,0:T(8,128)(2,1)} %pad_maximum_fusion), channel_id=1, source_target_pairs={{0,2},{1,3},{2,4},{3,5},{4,6},{5,7},{6,8},{7,9},{8,10},{9,11},{10,... | collective-permute-start | bytes 4718600 | tf_op jit(solution)/shard_map/ppermute | solution.py:17
  143.1 181.6 %collective-permute-start.2 = (bf16[2,384,1024]{2,1,0:T(8,128)(2,1)}, bf16[2,384,1024]{2,1,0:T(8,128)(2,1)}, u32[]{:S(2)}, u32[]{:S(2)}) collective-permute-start(bf16[2,384,1024]{2,1,0:T(8,128)(2,1)} %pad_maximum_fusion), channel_id=1, source_target_pairs={{0,1},{1,2},{2,3},{3,4},{4,5},{5,6},{6,7},{7,8},{8,9},{9,10},{10,1... | collective-permute-start | bytes 4718600 | tf_op jit(solution)/shard_map/ppermute | solution.py:17
  145.6 183.2 %collective-permute-start.3 = (bf16[2,384,1024]{2,1,0:T(8,128)(2,1)}, bf16[2,384,1024]{2,1,0:T(8,128)(2,1)}, u32[]{:S(2)}, u32[]{:S(2)}) collective-permute-start(bf16[2,384,1024]{2,1,0:T(8,128)(2,1)} %pad_maximum_fusion), channel_id=1, source_target_pairs={{1,0},{2,1},{3,2},{4,3},{5,4},{6,5},{7,6},{8,7},{9,8},{10,9},{11,1... | collective-permute-start | bytes 4718600 | tf_op jit(solution)/shard_map/ppermute | solution.py:17
  149.9 181.7 %collective-permute-start.4 = (bf16[2,384,1024]{2,1,0:T(8,128)(2,1)}, bf16[2,384,1024]{2,1,0:T(8,128)(2,1)}, u32[]{:S(2)}, u32[]{:S(2)}) collective-permute-start(bf16[2,384,1024]{2,1,0:T(8,128)(2,1)} %pad_maximum_fusion), channel_id=1, source_target_pairs={{2,0},{3,1},{4,2},{5,3},{6,4},{7,5},{8,6},{9,7},{10,8},{11,9},{12,... | collective-permute-start | bytes 4718600 | tf_op jit(solution)/shard_map/ppermute | solution.py:17
  291.9 42.4 %collective-permute-start.5 = (bf16[2,384,1024]{2,1,0:T(8,128)(2,1)}, bf16[2,384,1024]{2,1,0:T(8,128)(2,1)}, u32[]{:S(2)}, u32[]{:S(2)}) collective-permute-start(bf16[2,384,1024]{2,1,0:T(8,128)(2,1)} %pad_maximum_fusion), channel_id=1, source_target_pairs={{3,0},{4,1},{5,2},{6,3},{7,4},{8,5},{9,6},{10,7},{11,8},{12,9},{13... | collective-permute-start | bytes 4718600 | tf_op jit(solution)/shard_map/ppermute | solution.py:17
  309.1 135.4 %all-to-all-start = ((bf16[64,3,8192]{2,1,0:T(4,128)(2,1)}), bf16[64,3,8192]{2,1,0:T(4,128)(2,1)}, u32[]{:S(2)}, u32[]{:S(2)}) async-start(bf16[64,3,8192]{2,1,0:T(4,128)(2,1)} %all_to_all.8), calls=%async_computation | async-start | bytes 8388608 | tf_op jit(solution)/shard_map/all_to_all | solution.py:141
  321.9 5.5 %copy-start.3 = (bf16[384,1024]{1,0:T(8,128)(2,1)S(1)}, bf16[384,1024]{1,0:T(8,128)(2,1)}, u32[]{:S(2)}) copy-start(bf16[384,1024]{1,0:T(8,128)(2,1)} %copy-done.2) | copy-start | bytes 2359300
  321.9 5.5 %copy-start.5 = (bf16[1,384,1024]{2,1,0:T(8,128)(2,1)S(1)}, bf16[1,384,1024]{2,1,0:T(8,128)(2,1)}, u32[]{:S(2)}) copy-start(bf16[1,384,1024]{2,1,0:T(8,128)(2,1)} %copy-done.4) | copy-start | bytes 2359300
  354.5 8.4 %copy-start.7 = (bf16[8,384,2,64]{1,3,2,0:T(8,128)(2,1)S(1)}, bf16[8,384,2,64]{1,3,2,0:T(8,128)(2,1)}, u32[]{:S(2)}) copy-start(bf16[8,384,2,64]{1,3,2,0:T(8,128)(2,1)} %custom-call.5) | copy-start | bytes 2359300
Sparse Core Ops, SparseCore 0:
  19.3 85.4 all-gather.2
  292.0 87.7 all-gather.4
where the time goes:
time: 461 us; the launch traced here: 459 us
  blocking collectives  151 us (33%)
  local copies, waits for them, and re-layouts  144 us (31%)
  matrix products  62.8 us (14%)
  other arithmetic  40.6 us (9%)
  starting transfers between devices  29.3 us (6%)
  waiting for transfers between devices  16.1 us (3%)
  between operations  14.3 us (3%)
    all_gather x1, blocking collectives, per_device(): lax.all_gather(output_weight, 'grp', axis=1, tiled=True)  139 us
    gather x17, local copies, waits for them, and re-layouts, positions_of(): starts = jnp.searchsorted(segment_ids, own_ids, side='left')  62.7 us
    dot_general x8, matrix products, one_pair(): jnp.einsum('nts,snd->tnd', weights, value_pair, preferred_element_type=jn...  28.5 us
    slice x3, local copies, waits for them, and re-layouts, per_device(): mixed_rows = attend_pairs(queries, window[0], window[1], allowed, H)  26 us
    dot_general x8, matrix products, pair_scores(): jnp.einsum('tnd,snd->nts', query_pair, key_pair, preferred_element_type=j...  25.7 us
    ppermute x6, starting transfers between devices, shifted(): lax.ppermute(value, axis, [(source, source + steps) for source in range(i...  19.1 us
    reduce_sum x8, other arithmetic, one_pair(): row_total = jnp.sum(exponent, axis=-1)  18.5 us
    all_gather x1, waiting for transfers between devices, per_device(): lax.all_gather(input_cols, 'tok', axis=0, tiled=True)  16 us
  transfers between devices with their start and end apart: 9, of which 1 were waited for; matrix products, arithmetic and copies ran while one was open for 45% of the time, Pallas kernels for 0%

commit v1 on v0

--- a/solution.py
+++ b/solution.py
@@ -9,6 +9,11 @@
 NEG_FILL = -1e30
 ROPE_BASE = 160000.0
 EPSILON = 1e-05
+
+
+def gather_over(x, mesh_axis, dim):
+    outgoing = jnp.stack([x] * lax.axis_size(mesh_axis))
+    return jnp.concatenate(lax.all_to_all(outgoing, mesh_axis, 0, 0), axis=dim)
 
 
 def shifted(value, axis, steps):
@@ -96,11 +101,7 @@
         lax.all_gather(output_weight, "grp", axis=1, tiled=True),
     )
     section = normed
-    joined = jnp.dot(
-        section,
-        lax.all_gather(input_cols, "tok", axis=0, tiled=True),
-        preferred_element_type=jnp.float32,
-    )
+    joined = jnp.dot(section, gather_over(input_cols, "tok", 0), preferred_element_type=jnp.float32)
     own_ids = lax.dynamic_slice_in_dim(segment_ids, first_row, row_count, 0)
     positions = positions_of(segment_ids, own_ids, first_row)
     queries = rotate(joined[:, :model_width], positions, H)

time: 461 us -> 530 us (1.15)
  waiting for transfers between devices: 16.1 us -> 91.6 us
  local copies, waits for them, and re-layouts: 144 us -> 126 us
  starting transfers between devices: 29.3 us -> 43.6 us
    all_to_all x0 -> x1, waiting for transfers between devices: none -> 91.5 us  [gather_over(): return jnp.concatenate(lax.all_to_all(outgoing, mesh_axis, 0, 0), axis=dim)]
    gather x17, local copies, waits for them, and re-layouts: 62.7 us -> 43.1 us  [positions_of(): starts = jnp.searchsorted(segment_ids, own_ids, side='left')]
    all_gather x1 -> x0, waiting for transfers between devices: 16 us -> none  [per_device(): lax.all_gather(input_cols, 'tok', axis=0, tiled=True)]
    all_to_all x0 -> x1, starting transfers between devices: none -> 15.5 us  [gather_over(): return jnp.concatenate(lax.all_to_all(outgoing, mesh_axis, 0, 0), axis=dim)]
    unnamed x29 -> x27, local copies, waits for them, and re-layouts: 14.6 us -> 14.6 us
  transfers between devices with their start and end apart: 9 -> 9, of which waited for: 1 -> 1; matrix products, arithmetic and copies ran while one was open for 45% -> 35% of each run, Pallas kernels for 0% -> 0%
where the time goes in v1:
time: 530 us; the launch traced here: 528 us
  blocking collectives  149 us (28%)
  local copies, waits for them, and re-layouts  126 us (24%)
  waiting for transfers between devices  91.6 us (17%)
  matrix products  62.8 us (12%)
  starting transfers between devices  43.6 us (8%)
  other arithmetic  39.9 us (8%)
  between operations  14.3 us (3%)
    all_gather x1, blocking collectives, per_device(): lax.all_gather(output_weight, 'grp', axis=1, tiled=True)  138 us
    all_to_all x1, waiting for transfers between devices, gather_over(): return jnp.concatenate(lax.all_to_all(outgoing, mesh_axis, 0, 0), axis=dim)  91.5 us
    gather x17, local copies, waits for them, and re-layouts, positions_of(): starts = jnp.searchsorted(segment_ids, own_ids, side='left')  43.1 us
    dot_general x8, matrix products, one_pair(): jnp.einsum('nts,snd->tnd', weights, value_pair, preferred_element_type=jn...  28.5 us
    dot_general x8, matrix products, pair_scores(): jnp.einsum('tnd,snd->nts', query_pair, key_pair, preferred_element_type=j...  25.6 us
    slice x3, local copies, waits for them, and re-layouts, per_device(): mixed_rows = attend_pairs(queries, window[0], window[1], allowed, H)  25.5 us
    ppermute x6, starting transfers between devices, shifted(): lax.ppermute(value, axis, [(source, source + steps) for source in range(i...  19 us
    reduce_sum x8, other arithmetic, one_pair(): row_total = jnp.sum(exponent, axis=-1)  18.5 us
  transfers between devices with their start and end apart: 9, of which 1 were waited for; matrix products, arithmetic and copies ran while one was open for 35% of the time, Pallas kernels for 0%

profile of v1, /device:TPU:1, one launch (start us, length us, event | category | flops | bytes accessed | tf_op | source)
XLA Modules:
  0.0 528.5 jit_solution(6284467351711148417)
XLA Ops:
  7.2 10.4 %all_gather.9 = bf16[16,3072]{1,0:T(8,128)(2,1)S(1)} all-gather(bf16[16,768]{1,0:T(8,128)(2,1)} %param.12), channel_id=1, replica_groups=mesh['tok'=64,'grp'=4] {'grp'}, dimensions={1}, use_global_device_ids=true | all-gather | bytes 122880 | tf_op jit(solution)/shard_map/all_gather | solution.py:100
  17.6 3.4 stack.8
  21.0 15.5 %all-to-all-start = ((bf16[64,16,3072]{2,1,0:T(8,128)(2,1)}), bf16[64,16,3072]{2,1,0:T(8,128)(2,1)}, u32[]{:S(2)}, u32[]{:S(2)}) async-start(bf16[64,16,3072]{2,1,0:T(8,128)(2,1)} %stack.8), calls=%async_computation | async-start | bytes 12582912 | tf_op jit(solution)/shard_map/all_to_all | solution.py:16
  36.7 44.7 %while.36 = (s32[]{:T(128)}, u32[384]{0:T(512)S(1)}, u32[384]{0:T(512)S(1)}, s32[98304]{0:T(1024)S(1)}, s32[384]{0:T(512)S(1)}, /*index=5*/s32[]{:T(128)}, s32[]{:T(128)}, s32[]{}) while((s32[]{:T(128)}, u32[384]{0:T(512)S(1)}, u32[384]{0:T(512)S(1)}, s32[98304]{0:T(1024)S(1)}, s32[384]{0:T(512)S(1)}, /*index=5*/s32[]{:T(128)}, ...), condition=%wide.region_3.4_spmd.clone, body=%wide.region_2.3_spmd.clone.sunk | while | flops 7940 | bytes 31085 | solution.py:50
  36.7 2.5 gather_fusion
  39.3 2.5 gather_fusion
  42.0 2.5 gather_fusion
  44.6 2.5 gather_fusion
  47.2 2.5 gather_fusion
  49.9 2.5 gather_fusion
  52.5 2.5 gather_fusion
  55.1 2.5 gather_fusion
  57.8 2.5 gather_fusion
  60.4 2.5 gather_fusion
  63.0 2.5 gather_fusion
  65.7 2.5 gather_fusion
  68.3 2.5 gather_fusion
  70.9 2.5 gather_fusion
  73.6 2.5 gather_fusion
  76.2 2.5 gather_fusion
  78.8 2.5 gather_fusion
  85.8 91.5 %all-to-all-done = bf16[64,16,3072]{2,1,0:T(8,128)(2,1)} async-done(((bf16[64,16,3072]{2,1,0:T(8,128)(2,1)}), bf16[64,16,3072]{2,1,0:T(8,128)(2,1)}, u32[]{:S(2)}, u32[]{:S(2)}) %all-to-all-start) | async-done | bytes 6291488 | tf_op jit(solution)/shard_map/all_to_all | solution.py:16
  177.3 5.1 fusion.38
  185.7 3.3 copy.21
  189.1 3.1 copy.25
  196.3 3.1 copy.22
  199.4 3.0 copy.26
  202.5 4.6 add_convert_fusion
  208.4 4.0 collective-permute-start
  214.4 2.5 collective-permute-start.2
  216.9 4.3 collective-permute-start.3
  221.2 4.2 collective-permute-start.4
  225.4 138.1 %all_gather.10 = bf16[16,1024]{1,0:T(8,128)(2,1)} all-gather(bf16[16,256]{1,0:T(8,128)(2,1)S(1)} %copy-done.9), channel_id=1, replica_groups=mesh['tok'=64,'grp'=4] {'grp'}, dimensions={1}, use_global_device_ids=true | all-gather | bytes 40960 | tf_op jit(solution)/shard_map/all_gather | solution.py:101
  371.3 4.6 scatter_custom_fusion
  375.9 4.4 all_to_all.12
  380.3 9.0 %all-to-all-start.1 = ((bf16[64,3,8192]{2,1,0:T(4,128)(2,1)}), bf16[64,3,8192]{2,1,0:T(4,128)(2,1)}, u32[]{:S(2)}, u32[]{:S(2)}) async-start(bf16[64,3,8192]{2,1,0:T(4,128)(2,1)} %all_to_all.12), calls=%async_computation.1 | async-start | bytes 8388608 | tf_op jit(solution)/shard_map/all_to_all | solution.py:142
  389.3 2.7 constant_dynamic-update-slice_fusion.6
  392.1 2.9 constant_dynamic-update-slice_fusion.5
  394.9 2.7 constant_dynamic-update-slice_fusion.4
  399.0 2.8 constant_dynamic-update-slice_fusion.2
  401.8 2.6 constant_dynamic-update-slice_fusion.1
  404.4 2.7 constant_dynamic-update-slice_fusion
  407.1 9.6 %fusion.47 = (bf16[1,2688,1024]{2,1,0:T(8,128)(2,1)}, bf16[1,2688,1024]{2,1,0:T(8,128)(2,1)}) fusion(bf16[2,2688,1024]{2,1,0:T(8,128)(2,1)} %constant_dynamic-update-slice_fusion), kind=kLoop, calls=%fused_computation.79 | loop fusion | bytes 22020096 | tf_op jit(solution)/shard_map/slice | solution.py:122
  416.7 7.9 %copy.28 = bf16[1,2688,1024]{1,2,0:T(8,128)(2,1)} copy(bf16[1,2688,1024]{2,1,0:T(8,128)(2,1)} %get-tuple-element.165) | data formatting | bytes 11010048 | tf_op jit(solution)/shard_map/slice | solution.py:122
  424.6 8.0 %copy.23 = bf16[1,2688,1024]{1,2,0:T(8,128)(2,1)} copy(bf16[1,2688,1024]{2,1,0:T(8,128)(2,1)} %get-tuple-element.166) | data formatting | bytes 11010048 | tf_op jit(solution)/shard_map/slice | solution.py:122
  432.6 78.1 %while.35 = (s32[]{:T(128)}, bf16[8,384,2,64]{1,3,2,0:T(8,128)(2,1)S(1)}, bf16[8,2688,2,64]{1,3,2,0:T(8,128)(2,1)}, bf16[8,384,2,64]{1,3,2,0:T(8,128)(2,1)}, bf1...) while((s32[]{:T(128)}, ...), condition=%wide.region_7.8_spmd.clone, body=%wide.region_4.7_spmd.clone.sunk | while | flops 552270336 | bytes 30602324 | solution.py:85
  433.3 3.2 fusion.59
  438.8 3.6 fusion.61
  443.0 3.2 fusion.59
  448.5 3.6 fusion.61
  452.8 3.2 fusion.59
  458.3 3.6 fusion.61
  462.5 3.2 fusion.59
  468.1 3.6 fusion.61
  472.3 3.2 fusion.59
  477.8 3.6 fusion.61
  482.1 3.2 fusion.59
  487.6 3.6 fusion.61
  491.8 3.2 fusion.59
  497.3 3.6 fusion.61
  501.6 3.2 fusion.59
  507.1 3.6 fusion.61
  510.7 3.5 convolution_convert_fusion
  514.2 7.4 %all_to_all.14 = bf16[192,8192]{1,0:T(8,128)(2,1)} reshape(bf16[64,3,8192]{2,1,0:T(4,128)(2,1)} %all-to-all-done.1) | data formatting | bytes 6291456 | tf_op jit(solution)/shard_map/all_to_all | solution.py:142
  (163 shorter events, 48.6 us)
Async XLA Ops:
  21.0 15.6 %copy-start = (s32[98304]{0:T(1024)S(1)}, s32[98304]{0:T(1024)}, u32[]{:S(2)}) copy-start(s32[98304]{0:T(1024)} %param.14) | copy-start | bytes 1179652
  21.0 156.3 %all-to-all-start = ((bf16[64,16,3072]{2,1,0:T(8,128)(2,1)}), bf16[64,16,3072]{2,1,0:T(8,128)(2,1)}, u32[]{:S(2)}, u32[]{:S(2)}) async-start(bf16[64,16,3072]{2,1,0:T(8,128)(2,1)} %stack.8), calls=%async_computation | async-start | bytes 12582912 | tf_op jit(solution)/shard_map/all_to_all | solution.py:16
  36.5 474.2 %all-gather.2.cloned.1.call-start = ((), (), s32[]{:S(2)}) async-start(), calls=%async_computation.2 | async-start | bytes 2129920 | tf_op jit(solution)/shard_map/all_gather | solution.py:126
  182.5 3.1 copy-start.1
  185.7 21.4 %copy-start.4 = (bf16[1,384,1024]{2,1,0:T(8,128)(2,1)}, bf16[1,384,1024]{2,1,0:T(8,128)(2,1)S(1)}, u32[]{:S(2)}) copy-start(bf16[1,384,1024]{2,1,0:T(8,128)(2,1)S(1)} %slice_bitcast_fusion) | copy-start | bytes 2359300
  192.1 2.2 copy-start.8
  207.1 161.6 %copy-start.2 = (bf16[384,1024]{1,0:T(8,128)(2,1)}, bf16[384,1024]{1,0:T(8,128)(2,1)S(1)}, u32[]{:S(2)}) copy-start(bf16[384,1024]{1,0:T(8,128)(2,1)S(1)} %get-tuple-element.168) | copy-start | bytes 2359300
  207.1 18.3 %copy-start.9 = (bf16[16,256]{1,0:T(8,128)(2,1)S(1)}, bf16[16,256]{1,0:T(8,128)(2,1)}, u32[]{:S(2)}) copy-start(bf16[16,256]{1,0:T(8,128)(2,1)} %param.13) | copy-start | bytes 24580
  207.1 158.7 %copy-start.10 = (s32[96,1]{0,1:T(1,128)S(1)}, s32[96,1]{0,1:T(1,128)}, u32[]{:S(2)}) copy-start(s32[96,1]{0,1:T(1,128)} %param.15) | copy-start | bytes 1156
  207.1 160.4 %copy-start.6 = (bf16[384,1024]{1,0:T(8,128)(2,1)S(1)}, bf16[384,1024]{1,0:T(8,128)(2,1)}, u32[]{:S(2)}) copy-start(bf16[384,1024]{1,0:T(8,128)(2,1)} %get-tuple-element.167) | copy-start | bytes 2359300
  208.4 155.2 %collective-permute-start = (bf16[2,384,1024]{2,1,0:T(8,128)(2,1)}, bf16[2,384,1024]{2,1,0:T(8,128)(2,1)}, u32[]{:S(2)}, u32[]{:S(2)}) collective-permute-start(bf16[2,384,1024]{2,1,0:T(8,128)(2,1)} %pad_maximum_fusion), channel_id=1, source_target_pairs={{0,3},{1,4},{2,5},{3,6},{4,7},{5,8},{6,9},{7,10},{8,11},{9,12},{10... | collective-permute-start | bytes 4718600 | tf_op jit(solution)/shard_map/ppermute | solution.py:22
  212.4 179.6 %collective-permute-start.1 = (bf16[2,384,1024]{2,1,0:T(8,128)(2,1)}, bf16[2,384,1024]{2,1,0:T(8,128)(2,1)}, u32[]{:S(2)}, u32[]{:S(2)}) collective-permute-start(bf16[2,384,1024]{2,1,0:T(8,128)(2,1)} %pad_maximum_fusion), channel_id=1, source_target_pairs={{0,2},{1,3},{2,4},{3,5},{4,6},{5,7},{6,8},{7,9},{8,10},{9,11},{10,... | collective-permute-start | bytes 4718600 | tf_op jit(solution)/shard_map/ppermute | solution.py:22
  214.4 180.5 %collective-permute-start.2 = (bf16[2,384,1024]{2,1,0:T(8,128)(2,1)}, bf16[2,384,1024]{2,1,0:T(8,128)(2,1)}, u32[]{:S(2)}, u32[]{:S(2)}) collective-permute-start(bf16[2,384,1024]{2,1,0:T(8,128)(2,1)} %pad_maximum_fusion), channel_id=1, source_target_pairs={{0,1},{1,2},{2,3},{3,4},{4,5},{5,6},{6,7},{7,8},{8,9},{9,10},{10,1... | collective-permute-start | bytes 4718600 | tf_op jit(solution)/shard_map/ppermute | solution.py:22
  216.9 182.1 %collective-permute-start.3 = (bf16[2,384,1024]{2,1,0:T(8,128)(2,1)}, bf16[2,384,1024]{2,1,0:T(8,128)(2,1)}, u32[]{:S(2)}, u32[]{:S(2)}) collective-permute-start(bf16[2,384,1024]{2,1,0:T(8,128)(2,1)} %pad_maximum_fusion), channel_id=1, source_target_pairs={{1,0},{2,1},{3,2},{4,3},{5,4},{6,5},{7,6},{8,7},{9,8},{10,9},{11,1... | collective-permute-start | bytes 4718600 | tf_op jit(solution)/shard_map/ppermute | solution.py:22
  221.2 180.6 %collective-permute-start.4 = (bf16[2,384,1024]{2,1,0:T(8,128)(2,1)}, bf16[2,384,1024]{2,1,0:T(8,128)(2,1)}, u32[]{:S(2)}, u32[]{:S(2)}) collective-permute-start(bf16[2,384,1024]{2,1,0:T(8,128)(2,1)} %pad_maximum_fusion), channel_id=1, source_target_pairs={{2,0},{3,1},{4,2},{5,3},{6,4},{7,5},{8,6},{9,7},{10,8},{11,9},{12,... | collective-permute-start | bytes 4718600 | tf_op jit(solution)/shard_map/ppermute | solution.py:22
  363.6 40.8 %collective-permute-start.5 = (bf16[2,384,1024]{2,1,0:T(8,128)(2,1)}, bf16[2,384,1024]{2,1,0:T(8,128)(2,1)}, u32[]{:S(2)}, u32[]{:S(2)}) collective-permute-start(bf16[2,384,1024]{2,1,0:T(8,128)(2,1)} %pad_maximum_fusion), channel_id=1, source_target_pairs={{3,0},{4,1},{5,2},{6,3},{7,4},{8,5},{9,6},{10,7},{11,8},{12,9},{13... | collective-permute-start | bytes 4718600 | tf_op jit(solution)/shard_map/ppermute | solution.py:22
  380.3 133.9 %all-to-all-start.1 = ((bf16[64,3,8192]{2,1,0:T(4,128)(2,1)}), bf16[64,3,8192]{2,1,0:T(4,128)(2,1)}, u32[]{:S(2)}, u32[]{:S(2)}) async-start(bf16[64,3,8192]{2,1,0:T(4,128)(2,1)} %all_to_all.12), calls=%async_computation.1 | async-start | bytes 8388608 | tf_op jit(solution)/shard_map/all_to_all | solution.py:142
  392.0 5.6 %copy-start.3 = (bf16[384,1024]{1,0:T(8,128)(2,1)S(1)}, bf16[384,1024]{1,0:T(8,128)(2,1)}, u32[]{:S(2)}) copy-start(bf16[384,1024]{1,0:T(8,128)(2,1)} %copy-done.2) | copy-start | bytes 2359300
  392.0 5.6 %copy-start.5 = (bf16[1,384,1024]{2,1,0:T(8,128)(2,1)S(1)}, bf16[1,384,1024]{2,1,0:T(8,128)(2,1)}, u32[]{:S(2)}) copy-start(bf16[1,384,1024]{2,1,0:T(8,128)(2,1)} %copy-done.4) | copy-start | bytes 2359300
  424.6 8.0 %copy-start.7 = (bf16[8,384,2,64]{1,3,2,0:T(8,128)(2,1)S(1)}, bf16[8,384,2,64]{1,3,2,0:T(8,128)(2,1)}, u32[]{:S(2)}) copy-start(bf16[8,384,2,64]{1,3,2,0:T(8,128)(2,1)} %custom-call.5) | copy-start | bytes 2359300
Sparse Core Ops, SparseCore 0:
  363.7 86.6 all-gather.1
